TPU v7x, 32 devices: a whole 2x2x4 slice. The times are simulated.
32 devices in a mesh: face: 4 (over z), strip: 8 (over y, x, core).
Axes of the slice: x: 2, y: 2, z: 4, core: 2. Of those that a mesh axis runs over, the one named last changes fastest.
Arguments:
- pixels_in: bfloat16 [4, 8, 64, 1024], P('face', 'strip'), may hold values from -6 to 6
- w_qkv: bfloat16 [1024, 3072], P(None, 'face'), may hold values from -0.1875 to 0.1875
- w_gate: bfloat16 [1024, 32], P(None, 'face'), may hold values from -0.1875 to 0.1875
- decay_rate: float32 [16], replicated, may hold values from 0.0005859375 to 0.05
- beta_bias: float32 [16], replicated, may hold values from -4 to 1
Outputs:
- mixed: bfloat16 [4, 8, 64, 1024], P('face', 'strip')
All inputs are finite; a program needn't handle non-finite values.
Results may differ from a plain program's by a relative error of at most 0.0069.
Values may be sent and summed in bfloat16 or wider, within the bound.
A program may use at most 192 MiB of HBM per device.

v0:
```python
import jax
import jax.numpy as jnp
from jax import lax
from jax.sharding import PartitionSpec as P

highest = lax.Precision.HIGHEST


def carried_in(part, axis, combine, identity):
    place = lax.axis_index(axis)
    gathered = jax.tree.map(lambda a: lax.all_gather(a, axis), part)
    state = jax.tree.map(lambda a, e: jnp.zeros_like(a) + jnp.asarray(e, a.dtype), part, identity)

    def one(turn, state):
        return combine(
            state, jax.tree.map(lambda a: lax.dynamic_index_in_dim(a, turn, 0, False), gathered)
        )

    return lax.fori_loop(0, place, one, state)


def unit_rows(tensor):
    return tensor / jnp.sqrt(jnp.sum(tensor * tensor, axis=-1, keepdims=True) + 1e-06)


def head_norm(tensor):
    normed = tensor / jnp.sqrt(jnp.mean(tensor * tensor, axis=-1, keepdims=True) + 1e-06)
    return normed.reshape(tensor.shape[0], -1)


def project(flat_px, w_full, gate_full):
    projected = jnp.dot(flat_px, w_full, preferred_element_type=jnp.float32).astype(jnp.bfloat16)
    gate_logits = jnp.dot(flat_px, gate_full, preferred_element_type=jnp.float32).astype(
        jnp.bfloat16
    )
    return (projected, gate_logits)


def unpack(projected, gate_logits, decay_rate, beta_bias):
    heads = decay_rate.shape[0]
    count = projected.shape[0]
    parts = projected.astype(jnp.float32).reshape(count, 3, heads, -1)
    logits = gate_logits.astype(jnp.float32)
    log_decay = -decay_rate[None, :] * jnp.exp(logits[:, :heads])
    strength = jax.nn.sigmoid(logits[:, heads:] + beta_bias[None, :])
    return (unit_rows(parts[:, 0]), unit_rows(parts[:, 1]), parts[:, 2], log_decay, strength)


def group_terms(queries, key_rows, val_rows, log_decay, strength):
    span = queries.shape[1]
    width = queries.shape[2]
    cumulative = jnp.cumsum(log_decay, axis=1)
    gap_log = cumulative[:, :, None] - cumulative[:, None, :]
    row_ids = lax.broadcasted_iota(jnp.int32, (span, span), 0)
    col_ids = lax.broadcasted_iota(jnp.int32, (span, span), 1)
    inclusive = row_ids >= col_ids
    strict = row_ids > col_ids
    within = jnp.where(inclusive, jnp.exp(jnp.where(inclusive, gap_log, 0.0)), 0.0)
    key_dot = jnp.einsum("hck,hjk->hcj", key_rows, key_rows, precision=highest)
    lower_part = jnp.where(strict, within * key_dot, 0.0) * strength[:, :, None]
    system = lower_part + jnp.eye(span, dtype=queries.dtype)
    scale_all = jnp.exp(cumulative)
    rhs_values = val_rows * strength[:, :, None]
    rhs_keys = key_rows * (strength * scale_all)[:, :, None]
    solved = lax.linalg.triangular_solve(
        system,
        jnp.concatenate([rhs_values, rhs_keys], axis=-1),
        left_side=True,
        lower=True,
        unit_diagonal=True,
    )
    new_values = solved[..., :width]
    mixing = solved[..., width:]
    scores = jnp.where(
        inclusive, within * jnp.einsum("hck,hjk->hcj", queries, key_rows, precision=highest), 0.0
    )
    tail_decay = jnp.exp(cumulative[:, -1:] - cumulative)
    weighted_keys = key_rows * tail_decay[:, :, None]
    end_scale = jnp.exp(cumulative[:, -1])
    transition = end_scale[:, None, None] * jnp.eye(width, dtype=queries.dtype) - jnp.einsum(
        "hck,hcj->hkj", mixing, weighted_keys, precision=highest
    )
    writes = jnp.einsum("hcv,hck->hvk", new_values, weighted_keys, precision=highest)
    effective_query = queries * scale_all[:, :, None] - jnp.einsum(
        "hcj,hjk->hck", scores, mixing, precision=highest
    )
    local_out = jnp.einsum("hcj,hjv->hcv", scores, new_values, precision=highest)
    return (local_out, effective_query, transition, writes)


def to_blocks(queries, key_rows, val_rows, log_decay, strength):
    count = queries.shape[0] // 64

    def shape_four(tensor):
        return tensor.reshape(count, 64, tensor.shape[1], tensor.shape[2]).transpose(0, 2, 1, 3)

    def shape_three(tensor):
        return tensor.reshape(count, 64, tensor.shape[1]).transpose(0, 2, 1)

    return (
        shape_four(queries),
        shape_four(key_rows),
        shape_four(val_rows),
        shape_three(log_decay),
        shape_three(strength),
    )


def from_blocks(outputs):
    count, heads, span, width = outputs.shape
    return outputs.transpose(0, 2, 1, 3).reshape(count * span, heads, width)


def carried(prefix, local_state, eye_block, zero_state):

    def compose(earlier, later):
        joined_map = jnp.einsum("hkj,hjl->hkl", earlier[0], later[0], precision=highest)
        joined_state = (
            jnp.einsum("hvk,hkj->hvj", earlier[1], later[0], precision=highest) + later[1]
        )
        return (joined_map, joined_state)

    _, incoming = carried_in((prefix, local_state), "strip", compose, (eye_block, zero_state))
    return incoming


def strip_scan(queries, key_rows, val_rows, log_decay, strength):
    blocks = to_blocks(queries, key_rows, val_rows, log_decay, strength)
    heads = queries.shape[1]
    width = queries.shape[2]
    eye_block = jnp.broadcast_to(jnp.eye(width, dtype=jnp.float32), (heads, width, width))
    zero_state = jnp.zeros((heads, width, width), jnp.float32)

    def advance_local(carry, block_in):
        carry_state, prefix = carry
        local_out, effective_query, transition, writes = group_terms(*block_in)
        outputs = local_out + jnp.einsum(
            "hck,hvk->hcv", effective_query, carry_state, precision=highest
        )
        lifted = jnp.einsum("hck,hjk->hcj", effective_query, prefix, precision=highest)
        carry_state = (
            jnp.einsum("hvk,hkj->hvj", carry_state, transition, precision=highest) + writes
        )
        prefix = jnp.einsum("hkj,hjl->hkl", prefix, transition, precision=highest)
        return ((carry_state, prefix), (outputs, lifted))

    (local_state, prefix), (outputs, lifted) = lax.scan(
        advance_local, (zero_state, eye_block), blocks
    )
    incoming = carried(prefix, local_state, eye_block, zero_state)
    outputs = outputs + jnp.einsum("nhcj,hvj->nhcv", lifted, incoming, precision=highest)
    return from_blocks(outputs)


def on_device(pixels_in, w_qkv, w_gate, decay_rate, beta_bias):
    w_full, gate_full = (
        lax.all_gather(w_qkv, "face", axis=1, tiled=True),
        lax.all_gather(w_gate, "face", axis=1, tiled=True),
    )
    rows_here = pixels_in.shape[1]
    width_cols = pixels_in.shape[2]
    features = pixels_in.shape[3]
    n_strip = lax.axis_size("strip")
    cols_here = width_cols // n_strip
    tall_rows = rows_here * n_strip
    plane = pixels_in.reshape(rows_here, width_cols, features)
    projected, gate_logits = project(
        plane.reshape(rows_here * width_cols, features), w_full, gate_full
    )
    row_out = strip_scan(*unpack(projected, gate_logits, decay_rate, beta_bias))
    arrived_proj, arrived_gates = (
        lax.all_to_all(
            projected.reshape(rows_here, width_cols, -1),
            "strip",
            split_axis=1,
            concat_axis=0,
            tiled=True,
        ),
        lax.all_to_all(
            gate_logits.reshape(rows_here, width_cols, -1),
            "strip",
            split_axis=1,
            concat_axis=0,
            tiled=True,
        ),
    )
    col_proj = arrived_proj.swapaxes(0, 1).reshape(tall_rows * cols_here, -1)
    col_gates = arrived_gates.swapaxes(0, 1).reshape(tall_rows * cols_here, -1)
    col_out = strip_scan(*unpack(col_proj, col_gates, decay_rate, beta_bias))
    col_mixed = head_norm(col_out).astype(jnp.bfloat16)
    col_tall = col_mixed.reshape(cols_here, tall_rows, -1).swapaxes(0, 1)
    returned = lax.all_to_all(col_tall, "strip", split_axis=0, concat_axis=1, tiled=True)
    row_mixed = head_norm(row_out).reshape(rows_here, width_cols, -1)
    mixed = (row_mixed + returned.astype(jnp.float32)).astype(jnp.bfloat16)
    return mixed[None]


def solution(mesh):
    in_specs = (P("face", "strip", None, None), P(None, "face"), P(None, "face"), P(), P())
    out_specs = P("face", "strip", None, None)
    return jax.shard_map(
        on_device, mesh=mesh, in_specs=in_specs, out_specs=out_specs, check_vma=False
    )
```

profile of v0, /device:TPU:0, one launch (start us, length us, event | category | flops | bytes accessed | tf_op | source)
XLA Modules:
  0.0 444.6 jit_solution(4246070837941400303)
XLA Ops:
  7.3 15.1 %all_gather.30 = bf16[1024,32]{0,1:T(8,128)(2,1)S(1)} all-gather(bf16[1024,8]{0,1:T(8,128)(2,1)} %param.13), channel_id=1, replica_groups=mesh['face'=4,'strip'=8] {'face'}, dimensions={1}, use_global_device_ids=true | all-gather | bytes 81920 | tf_op jit(solution)/shard_map/all_gather | solution.py:158
  24.7 3.7 all-to-all-start
  29.4 3.8 all-to-all-done
  35.7 91.3 %all-gather.10.cloned.1.call-done = bf16[1024,3072]{1,0:T(8,128)(2,1)} async-done(((bf16[1024,768]{1,0:T(8,128)(2,1)}), bf16[1024,3072]{1,0:T(8,128)(2,1)}) %all-gather.10.cloned.1.call-update) | async-done | bytes 6291472 | tf_op jit(solution)/shard_map/all_gather | solution.py:157
  127.0 4.0 convolution_convert_fusion
  134.1 78.6 %custom-call.4 = f32[16,1,64,64]{2,3,1,0:T(8,128)S(1)} custom-call(f32[16,1,64,64]{3,2,1,0:T(8,128)S(1)} %fusion.19), custom_call_target="InvertDiagBlocksLowerTriangular" | custom-call | tf_op jit(solution)/shard_map/while/body/eval_jaxpr/triangular_solve/custom-call.1 | solution.py:65
  214.4 1.4 convolution_subtract_fusion.2
  215.8 1.4 fusion.67
  218.2 2.1 convolution_add_fusion.2
  220.9 3.0 reduce.11
  224.9 3.6 all-to-all-start.1
  229.7 7.1 %all-to-all-done.1 = bf16[8,2,12288]{2,1,0:T(2,128)(2,1)S(1)} async-done(((bf16[8,2,12288]{2,1,0:T(2,128)(2,1)}), bf16[8,2,12288]{2,1,0:T(2,128)(2,1)S(1)}, u32[]{:S(2)}, u32[]{:S(2)}) %all-to-all-start.1) | async-done | bytes 393248 | tf_op jit(solution)/shard_map/all_to_all | solution.py:172
  240.5 2.2 fusion.23
  242.7 79.3 %custom-call.5 = f32[16,1,64,64]{2,3,1,0:T(8,128)} custom-call(f32[16,1,64,64]{3,2,1,0:T(8,128)S(1)} %fusion.23), custom_call_target="InvertDiagBlocksLowerTriangular" | custom-call | tf_op jit(solution)/shard_map/while/body/eval_jaxpr/triangular_solve/custom-call.1 | solution.py:65
  322.5 2.2 fusion.31
  324.8 1.4 convolution_subtract_fusion
  331.3 1.9 convolution_subtract_fusion.3
  333.8 2.1 convolution_add_fusion
  336.9 1.7 fusion.65
  344.4 2.1 fusion.41
  346.7 17.2 %all-gather.16.cloned.1.call-done = f32[128,64,64]{2,1,0:T(8,128)} async-done(((f32[16,64,64]{2,1,0:T(8,128)}), f32[128,64,64]{2,1,0:T(8,128)}) %all-gather.16.cloned.1.call-update) | async-done | bytes 2097168 | tf_op jit(solution)/shard_map/all_gather | solution.py:11
  363.9 38.3 %all-gather.18.cloned.1.call-done = f32[128,64,64]{2,1,0:T(8,128)} async-done(((f32[16,64,64]{2,1,0:T(8,128)}), f32[128,64,64]{2,1,0:T(8,128)}) %all-gather.18.cloned.1.call-update) | async-done | bytes 2097168 | tf_op jit(solution)/shard_map/all_gather | solution.py:11
  405.1 26.5 %all-to-all-start.2 = ((bf16[8,8,1024]{2,1,0:T(8,128)(2,1)}), bf16[8,8,1024]{2,1,0:T(8,128)(2,1)S(1)}, u32[]{:S(2)}, u32[]{:S(2)}) async-start(bf16[8,8,1024]{2,1,0:T(8,128)(2,1)} %copy.134), calls=%async_computation.2 | async-start | bytes 262144 | tf_op jit(solution)/shard_map/all_to_all | solution.py:192
  432.1 5.0 %all-to-all-done.2 = bf16[8,8,1024]{2,1,0:T(8,128)(2,1)S(1)} async-done(((bf16[8,8,1024]{2,1,0:T(8,128)(2,1)}), bf16[8,8,1024]{2,1,0:T(8,128)(2,1)S(1)}, u32[]{:S(2)}, u32[]{:S(2)}) %all-to-all-start.2) | async-done | bytes 131104 | tf_op jit(solution)/shard_map/all_to_all | solution.py:192
  (132 shorter events, 35.3 us)
Async XLA Ops:
  6.5 15.9 %copy-start = (bf16[1,1,64,1024]{3,2,1,0:T(8,128)(2,1)S(1)}, bf16[1,1,64,1024]{3,2,1,0:T(8,128)(2,1)}, u32[]{:S(2)}) copy-start(bf16[1,1,64,1024]{3,2,1,0:T(8,128)(2,1)} %param.11) | copy-start | bytes 393220
  6.5 120.5 %all-gather.10.cloned.1.call-start = ((), (), s32[]{:S(2)}) async-start(), calls=%async_computation.3 | async-start | bytes 7864320 | tf_op jit(solution)/shard_map/all_gather | solution.py:157
  24.7 8.4 %all-to-all-start = ((bf16[8,2,128]{2,1,0:T(2,128)(2,1)}), bf16[8,2,128]{2,1,0:T(2,128)(2,1)S(1)}, u32[]{:S(2)}, u32[]{:S(2)}) async-start(bf16[8,2,128]{2,1,0:T(2,128)(2,1)} %reshape.328), calls=%async_computation | async-start | bytes 8192 | tf_op jit(solution)/shard_map/all_to_all | solution.py:179
  28.5 315.7 %all-gather.12.cloned.1.call-start = ((), (), s32[]{:S(2)}) async-start(), calls=%async_computation.4 | async-start | bytes 4718592 | tf_op jit(solution)/shard_map/all_gather | solution.py:11
  28.5 104.1 %copy-start.14 = (pred[64,64]{1,0:T(8,128)(4,1)}, pred[64,64]{1,0:T(8,128)(4,1)S(1)}, u32[]{:S(2)}) copy-start(pred[64,64]{1,0:T(8,128)(4,1)S(1)} %get-tuple-element.250) | copy-start | bytes 12292
  28.6 187.3 %copy-start.7 = (f32[64,64]{1,0:T(8,128)}, f32[64,64]{1,0:T(8,128)S(1)}, u32[]{:S(2)}) copy-start(f32[64,64]{1,0:T(8,128)S(1)} %get-tuple-element.251) | copy-start | bytes 49156
  28.6 104.0 %copy-start.19 = (pred[64,64]{1,0:T(8,128)(4,1)}, pred[64,64]{1,0:T(8,128)(4,1)S(1)}, u32[]{:S(2)}) copy-start(pred[64,64]{1,0:T(8,128)(4,1)S(1)} %get-tuple-element.248) | copy-start | bytes 12292
  28.7 104.0 %copy-start.20 = (pred[64,64]{1,0:T(8,128)(4,1)}, pred[64,64]{1,0:T(8,128)(4,1)S(1)}, u32[]{:S(2)}) copy-start(pred[64,64]{1,0:T(8,128)(4,1)S(1)} %get-tuple-element.249) | copy-start | bytes 12292
  28.7 104.0 %copy-start.13 = (f32[64,64]{1,0:T(8,128)}, f32[64,64]{1,0:T(8,128)S(1)}, u32[]{:S(2)}) copy-start(f32[64,64]{1,0:T(8,128)S(1)} %fusion.79) | copy-start | bytes 49156
  132.7 85.5 %copy-start.11 = (f32[64,16]{0,1:T(8,128)}, f32[64,16]{0,1:T(8,128)S(1)}, u32[]{:S(2)}) copy-start(f32[64,16]{0,1:T(8,128)S(1)} %add_sqrt_fusion.4) | copy-start | bytes 12292
  217.2 126.9 %all-gather.14.cloned.1.call-start = ((), (), s32[]{:S(2)}) async-start(), calls=%async_computation.5 | async-start | bytes 4718592 | tf_op jit(solution)/shard_map/all_gather | solution.py:11
  224.9 11.9 %all-to-all-start.1 = ((bf16[8,2,12288]{2,1,0:T(2,128)(2,1)}), bf16[8,2,12288]{2,1,0:T(2,128)(2,1)S(1)}, u32[]{:S(2)}, u32[]{:S(2)}) async-start(bf16[8,2,12288]{2,1,0:T(2,128)(2,1)} %reshape.330), calls=%async_computation.1 | async-start | bytes 786432 | tf_op jit(solution)/shard_map/all_to_all | solution.py:172
  228.6 135.3 %all-gather.16.cloned.1.call-start = ((), (), s32[]{:S(2)}) async-start(), calls=%async_computation.6 | async-start | bytes 4718592 | tf_op jit(solution)/shard_map/all_gather | solution.py:11
  240.2 81.8 %copy-start.6 = (f32[64,1,16,64]{3,2,1,0:T(8,128)S(1)}, f32[64,1,16,64]{3,2,1,0:T(8,128)}, u32[]{:S(2)}) copy-start(f32[64,1,16,64]{3,2,1,0:T(8,128)} %get-tuple-element.220) | copy-start | bytes 786436
  240.3 81.8 %copy-start.9 = (f32[16,64]{1,0:T(8,128)S(1)}, f32[16,64]{1,0:T(8,128)}, u32[]{:S(2)}) copy-start(f32[16,64]{1,0:T(8,128)} %get-tuple-element.234) | copy-start | bytes 12292
  240.3 81.8 %copy-start.10 = (f32[16,64]{1,0:T(8,128)S(1)}, f32[16,64]{1,0:T(8,128)}, u32[]{:S(2)}) copy-start(f32[16,64]{1,0:T(8,128)} %get-tuple-element.235) | copy-start | bytes 12292
  240.3 84.5 %copy-start.8 = (f32[64,64]{1,0:T(8,128)S(1)}, f32[64,64]{1,0:T(8,128)}, u32[]{:S(2)}) copy-start(f32[64,64]{1,0:T(8,128)} %copy-done.7) | copy-start | bytes 49156
  240.3 84.5 %copy-start.17 = (f32[16,64]{1,0:T(8,128)S(1)}, f32[16,64]{1,0:T(8,128)}, u32[]{:S(2)}) copy-start(f32[16,64]{1,0:T(8,128)} %get-tuple-element.233) | copy-start | bytes 12292
  240.3 84.5 %copy-start.21 = (f32[16]{0:T(128)S(1)}, f32[16]{0:T(128)}, u32[]{:S(2)}) copy-start(f32[16]{0:T(128)} %exp.84) | copy-start | bytes 196
  242.7 85.9 %copy-start.3 = (f32[64,1,16,64]{3,2,1,0:T(8,128)S(1)}, f32[64,1,16,64]{3,2,1,0:T(8,128)}, u32[]{:S(2)}) copy-start(f32[64,1,16,64]{3,2,1,0:T(8,128)} %get-tuple-element.225) | copy-start | bytes 786436
  322.0 6.9 %copy-start.12 = (f32[64,16]{0,1:T(8,128)S(1)}, f32[64,16]{0,1:T(8,128)}, u32[]{:S(2)}) copy-start(f32[64,16]{0,1:T(8,128)} %copy-done.11) | copy-start | bytes 12292
  322.0 6.9 %copy-start.15 = (pred[64,64]{1,0:T(8,128)(4,1)S(1)}, pred[64,64]{1,0:T(8,128)(4,1)}, u32[]{:S(2)}) copy-start(pred[64,64]{1,0:T(8,128)(4,1)} %copy-done.14) | copy-start | bytes 12292
  328.4 73.9 %all-gather.18.cloned.1.call-start = ((), (), s32[]{:S(2)}) async-start(), calls=%async_computation.7 | async-start | bytes 4718592 | tf_op jit(solution)/shard_map/all_gather | solution.py:11
  405.1 32.0 %all-to-all-start.2 = ((bf16[8,8,1024]{2,1,0:T(8,128)(2,1)}), bf16[8,8,1024]{2,1,0:T(8,128)(2,1)S(1)}, u32[]{:S(2)}, u32[]{:S(2)}) async-start(bf16[8,8,1024]{2,1,0:T(8,128)(2,1)} %copy.134), calls=%async_computation.2 | async-start | bytes 262144 | tf_op jit(solution)/shard_map/all_to_all | solution.py:192
  (6 other events, 23.6 us)
Sparse Core Ops, SparseCore 0:
  8.9 118.0 all-gather.9
  217.4 39.1 all-gather.11
  258.4 37.3 all-gather.13
  328.5 35.3 all-gather.15
  365.7 36.5 all-gather.17
where the time goes:
time: 453 us; the launch traced here: 445 us
  other arithmetic  168 us (37%)
  waiting for transfers between devices  164 us (36%)
  matrix products  37.2 us (8%)
  starting transfers between devices  35 us (8%)
  blocking collectives  15.1 us (3%)
  between operations  14 us (3%)
  local copies, waits for them, and re-layouts  11.4 us (3%)
    another operation x5, other arithmetic, group_terms(): lax.linalg.triangular_solve(system, jnp.concatenate([rhs_values, rhs_keys...  158 us
    all_gather x1, waiting for transfers between devices, on_device(): lax.all_gather(w_qkv, 'face', axis=1, tiled=True)  91.3 us
    all_gather x4, waiting for transfers between devices, carried_in(): gathered = jax.tree.map(lambda a: lax.all_gather(a, axis), part)  55.6 us
    all_to_all x1, starting transfers between devices, on_device(): lax.all_to_all(col_tall, 'strip', split_axis=0, concat_axis=1, tiled=True)  26.5 us
    all_gather x1, blocking collectives, on_device(): lax.all_gather(w_gate, 'face', axis=1, tiled=True)  15.1 us
  transfers between devices with their start and end apart: 8, of which 6 were waited for; matrix products, arithmetic and copies ran while one was open for 27% of the time, Pallas kernels for 0%

commit v1 on v0

--- a/solution.py
+++ b/solution.py
@@ -154,7 +154,9 @@
 
 def on_device(pixels_in, w_qkv, w_gate, decay_rate, beta_bias):
     w_full, gate_full = (
-        lax.all_gather(w_qkv, "face", axis=1, tiled=True),
+        jnp.concatenate(
+            lax.all_to_all(jnp.stack([w_qkv] * lax.axis_size("face")), "face", 0, 0), axis=1
+        ),
         lax.all_gather(w_gate, "face", axis=1, tiled=True),
     )
     rows_here = pixels_in.shape[1]

time: 453 us -> 508 us (1.12)
  waiting for transfers between devices: 164 us -> 208 us
  local copies, waits for them, and re-layouts: 11.4 us -> 16.6 us
    all_to_all x0 -> x1, waiting for transfers between devices: none -> 136 us  [on_device(): lax.all_to_all(jnp.stack([w_qkv] * lax.axis_size('face')), 'face', 0, 0)]
    all_gather x1 -> x0, waiting for transfers between devices: 91.3 us -> none  [on_device(): lax.all_gather(w_qkv, 'face', axis=1, tiled=True)]
    all_to_all x0 -> x1, starting transfers between devices: none -> 5.38 us  [on_device(): lax.all_to_all(jnp.stack([w_qkv] * lax.axis_size('face')), 'face', 0, 0)]
  transfers between devices with their start and end apart: 8 -> 8, of which waited for: 6 -> 6; matrix products, arithmetic and copies ran while one was open for 27% -> 24% of each run, Pallas kernels for 0% -> 0%
where the time goes in v1:
time: 508 us; the launch traced here: 498 us
  waiting for transfers between devices  208 us (41%)
  other arithmetic  167 us (33%)
  starting transfers between devices  39.6 us (8%)
  matrix products  36.8 us (7%)
  local copies, waits for them, and re-layouts  16.6 us (3%)
  blocking collectives  15.3 us (3%)
  between operations  14.3 us (3%)
    another operation x5, other arithmetic, group_terms(): lax.linalg.triangular_solve(system, jnp.concatenate([rhs_values, rhs_keys...  157 us
    all_to_all x1, waiting for transfers between devices, on_device(): lax.all_to_all(jnp.stack([w_qkv] * lax.axis_size('face')), 'face', 0, 0)  136 us
    all_gather x4, waiting for transfers between devices, carried_in(): gathered = jax.tree.map(lambda a: lax.all_gather(a, axis), part)  56.4 us
    all_to_all x1, starting transfers between devices, on_device(): lax.all_to_all(col_tall, 'strip', split_axis=0, concat_axis=1, tiled=True)  26.5 us
    all_gather x1, blocking collectives, on_device(): lax.all_gather(w_gate, 'face', axis=1, tiled=True)  15.3 us
  transfers between devices with their start and end apart: 8, of which 6 were waited for; matrix products, arithmetic and copies ran while one was open for 24% of the time, Pallas kernels for 0%

profile of v1, /device:TPU:0, one launch (start us, length us, event | category | flops | bytes accessed | tf_op | source)
XLA Modules:
  0.0 498.2 jit_solution(10281778399850468841)
XLA Ops:
  6.5 15.3 %all_gather.27 = bf16[1024,32]{0,1:T(8,128)(2,1)S(1)} all-gather(bf16[1024,8]{0,1:T(8,128)(2,1)} %param.13), channel_id=1, replica_groups=mesh['face'=4,'strip'=8] {'face'}, dimensions={1}, use_global_device_ids=true | all-gather | bytes 81920 | tf_op jit(solution)/shard_map/all_gather | solution.py:160
  24.1 3.7 all-to-all-start.1
  27.8 1.7 copy.102
  29.6 2.9 all-to-all-done.1
  32.5 3.4 stack.2
  35.9 5.4 %all-to-all-start = ((bf16[4,1024,768]{1,2,0:T(8,128)(2,1)}), bf16[4,1024,768]{1,2,0:T(8,128)(2,1)}, u32[]{:S(2)}, u32[]{:S(2)}) async-start(bf16[4,1024,768]{1,2,0:T(8,128)(2,1)} %stack.2), calls=%async_computation | async-start | bytes 12582912 | tf_op jit(solution)/shard_map/all_to_all | solution.py:158
  43.5 136.2 %all-to-all-done = bf16[4,1024,768]{1,2,0:T(8,128)(2,1)} async-done(((bf16[4,1024,768]{1,2,0:T(8,128)(2,1)}), bf16[4,1024,768]{1,2,0:T(8,128)(2,1)}, u32[]{:S(2)}, u32[]{:S(2)}) %all-to-all-start) | async-done | bytes 6291488 | tf_op jit(solution)/shard_map/all_to_all | solution.py:158
  179.7 4.8 convolution_convert_fusion
  187.6 78.6 %custom-call.4 = f32[16,1,64,64]{2,3,1,0:T(8,128)S(1)} custom-call(f32[16,1,64,64]{3,2,1,0:T(8,128)S(1)} %fusion.19), custom_call_target="InvertDiagBlocksLowerTriangular" | custom-call | tf_op jit(solution)/shard_map/while/body/eval_jaxpr/triangular_solve/custom-call.1 | solution.py:65
  269.9 2.1 convolution_add_fusion.2
  274.3 3.0 reduce.11
  278.3 3.5 all-to-all-start.2
  282.4 7.9 %all-to-all-done.2 = bf16[8,2,12288]{2,1,0:T(2,128)(2,1)S(1)} async-done(((bf16[8,2,12288]{2,1,0:T(2,128)(2,1)}), bf16[8,2,12288]{2,1,0:T(2,128)(2,1)S(1)}, u32[]{:S(2)}, u32[]{:S(2)}) %all-to-all-start.2) | async-done | bytes 393248 | tf_op jit(solution)/shard_map/all_to_all | solution.py:174
  294.0 2.0 fusion.23
  296.1 78.6 %custom-call.5 = f32[16,1,64,64]{2,3,1,0:T(8,128)S(1)} custom-call(f32[16,1,64,64]{3,2,1,0:T(8,128)S(1)} %fusion.23), custom_call_target="InvertDiagBlocksLowerTriangular" | custom-call | tf_op jit(solution)/shard_map/while/body/eval_jaxpr/triangular_solve/custom-call.1 | solution.py:65
  376.4 1.4 convolution_subtract_fusion
  379.3 2.1 convolution_add_fusion
  387.6 1.7 fusion.65
  390.6 2.3 fusion.11
  397.2 2.1 fusion.41
  399.3 18.0 %all-gather.15.cloned.1.call-done = f32[128,64,64]{2,1,0:T(8,128)} async-done(((f32[16,64,64]{2,1,0:T(8,128)}), f32[128,64,64]{2,1,0:T(8,128)}) %all-gather.15.cloned.1.call-update) | async-done | bytes 2097168 | tf_op jit(solution)/shard_map/all_gather | solution.py:11
  417.3 38.4 %all-gather.13.cloned.1.call-done = f32[128,64,64]{2,1,0:T(8,128)} async-done(((f32[16,64,64]{2,1,0:T(8,128)}), f32[128,64,64]{2,1,0:T(8,128)}) %all-gather.13.cloned.1.call-update) | async-done | bytes 2097168 | tf_op jit(solution)/shard_map/all_gather | solution.py:11
  458.5 26.5 %all-to-all-start.3 = ((bf16[8,8,1024]{2,1,0:T(8,128)(2,1)}), bf16[8,8,1024]{2,1,0:T(8,128)(2,1)S(1)}, u32[]{:S(2)}, u32[]{:S(2)}) async-start(bf16[8,8,1024]{2,1,0:T(8,128)(2,1)} %copy.137), calls=%async_computation.3 | async-start | bytes 262144 | tf_op jit(solution)/shard_map/all_to_all | solution.py:194
  485.7 4.8 all-to-all-done.3
  (137 shorter events, 37.3 us)
Async XLA Ops:
  6.5 15.3 %copy-start = (bf16[1,1,64,1024]{3,2,1,0:T(8,128)(2,1)S(1)}, bf16[1,1,64,1024]{3,2,1,0:T(8,128)(2,1)}, u32[]{:S(2)}) copy-start(bf16[1,1,64,1024]{3,2,1,0:T(8,128)(2,1)} %param.11) | copy-start | bytes 393220
  24.1 8.3 %all-to-all-start.1 = ((bf16[8,2,128]{2,1,0:T(2,128)(2,1)}), bf16[8,2,128]{2,1,0:T(2,128)(2,1)S(1)}, u32[]{:S(2)}, u32[]{:S(2)}) async-start(bf16[8,2,128]{2,1,0:T(2,128)(2,1)} %reshape.338), calls=%async_computation.1 | async-start | bytes 8192 | tf_op jit(solution)/shard_map/all_to_all | solution.py:181
  35.9 5.4 %copy-start.22 = (f32[16]{0:T(128)S(1)}, f32[16]{0:T(128)}, u32[]{:S(2)}) copy-start(f32[16]{0:T(128)} %param.14) | copy-start | bytes 196
  35.9 6.9 %copy-start.21 = (f32[16]{0:T(128)S(1)}, f32[16]{0:T(128)}, u32[]{:S(2)}) copy-start(f32[16]{0:T(128)} %param.15) | copy-start | bytes 196
  35.9 143.8 %all-to-all-start = ((bf16[4,1024,768]{1,2,0:T(8,128)(2,1)}), bf16[4,1024,768]{1,2,0:T(8,128)(2,1)}, u32[]{:S(2)}, u32[]{:S(2)}) async-start(bf16[4,1024,768]{1,2,0:T(8,128)(2,1)} %stack.2), calls=%async_computation | async-start | bytes 12582912 | tf_op jit(solution)/shard_map/all_to_all | solution.py:158
  41.3 355.6 %all-gather.11.cloned.1.call-start = ((), (), s32[]{:S(2)}) async-start(), calls=%async_computation.5 | async-start | bytes 4718592 | tf_op jit(solution)/shard_map/all_gather | solution.py:11
  41.4 144.8 %copy-start.11 = (f32[64,64]{1,0:T(8,128)}, f32[64,64]{1,0:T(8,128)S(1)}, u32[]{:S(2)}) copy-start(f32[64,64]{1,0:T(8,128)S(1)} %fusion.79) | copy-start | bytes 49156
  41.4 144.8 %copy-start.13 = (pred[64,64]{1,0:T(8,128)(4,1)}, pred[64,64]{1,0:T(8,128)(4,1)S(1)}, u32[]{:S(2)}) copy-start(pred[64,64]{1,0:T(8,128)(4,1)S(1)} %get-tuple-element.250) | copy-start | bytes 12292
  41.4 230.8 %copy-start.7 = (f32[64,64]{1,0:T(8,128)}, f32[64,64]{1,0:T(8,128)S(1)}, u32[]{:S(2)}) copy-start(f32[64,64]{1,0:T(8,128)S(1)} %get-tuple-element.251) | copy-start | bytes 49156
  41.5 144.7 %copy-start.18 = (pred[64,64]{1,0:T(8,128)(4,1)}, pred[64,64]{1,0:T(8,128)(4,1)S(1)}, u32[]{:S(2)}) copy-start(pred[64,64]{1,0:T(8,128)(4,1)S(1)} %get-tuple-element.248) | copy-start | bytes 12292
  41.5 144.7 %copy-start.20 = (pred[64,64]{1,0:T(8,128)(4,1)}, pred[64,64]{1,0:T(8,128)(4,1)S(1)}, u32[]{:S(2)}) copy-start(pred[64,64]{1,0:T(8,128)(4,1)S(1)} %get-tuple-element.249) | copy-start | bytes 12292
  272.0 124.9 %all-gather.9.cloned.1.call-start = ((), (), s32[]{:S(2)}) async-start(), calls=%async_computation.4 | async-start | bytes 4718592 | tf_op jit(solution)/shard_map/all_gather | solution.py:11
  278.3 12.0 %all-to-all-start.2 = ((bf16[8,2,12288]{2,1,0:T(2,128)(2,1)}), bf16[8,2,12288]{2,1,0:T(2,128)(2,1)S(1)}, u32[]{:S(2)}, u32[]{:S(2)}) async-start(bf16[8,2,12288]{2,1,0:T(2,128)(2,1)} %reshape.340), calls=%async_computation.2 | async-start | bytes 786432 | tf_op jit(solution)/shard_map/all_to_all | solution.py:174
  281.7 135.6 %all-gather.15.cloned.1.call-start = ((), (), s32[]{:S(2)}) async-start(), calls=%async_computation.7 | async-start | bytes 4718592 | tf_op jit(solution)/shard_map/all_gather | solution.py:11
  292.6 82.2 %copy-start.9 = (f32[16,64]{1,0:T(8,128)S(1)}, f32[16,64]{1,0:T(8,128)}, u32[]{:S(2)}) copy-start(f32[16,64]{1,0:T(8,128)} %get-tuple-element.234) | copy-start | bytes 12292
  293.7 81.0 %copy-start.6 = (f32[64,1,16,64]{3,2,1,0:T(8,128)S(1)}, f32[64,1,16,64]{3,2,1,0:T(8,128)}, u32[]{:S(2)}) copy-start(f32[64,1,16,64]{3,2,1,0:T(8,128)} %get-tuple-element.220) | copy-start | bytes 786436
  293.7 82.7 %copy-start.17 = (f32[16,64]{1,0:T(8,128)S(1)}, f32[16,64]{1,0:T(8,128)}, u32[]{:S(2)}) copy-start(f32[16,64]{1,0:T(8,128)} %get-tuple-element.233) | copy-start | bytes 12292
  293.7 82.7 %copy-start.23 = (f32[16]{0:T(128)S(1)}, f32[16]{0:T(128)}, u32[]{:S(2)}) copy-start(f32[16]{0:T(128)} %exp.84) | copy-start | bytes 196
  375.3 6.4 %copy-start.4 = (f32[64,1,16,64]{3,2,1,0:T(8,128)S(1)}, f32[64,1,16,64]{3,2,1,0:T(8,128)}, u32[]{:S(2)}) copy-start(f32[64,1,16,64]{3,2,1,0:T(8,128)} %get-tuple-element.225) | copy-start | bytes 786436
  381.4 74.3 %all-gather.13.cloned.1.call-start = ((), (), s32[]{:S(2)}) async-start(), calls=%async_computation.6 | async-start | bytes 4718592 | tf_op jit(solution)/shard_map/all_gather | solution.py:11
  387.6 6.4 %copy-start.5 = (f32[64,1,16,64]{3,2,1,0:T(8,128)S(1)}, f32[64,1,16,64]{3,2,1,0:T(8,128)}, u32[]{:S(2)}) copy-start(f32[64,1,16,64]{3,2,1,0:T(8,128)} %get-tuple-element.222) | copy-start | bytes 786436
  387.6 6.4 %copy-start.15 = (f32[16,64]{1,0:T(8,128)S(1)}, f32[16,64]{1,0:T(8,128)}, u32[]{:S(2)}) copy-start(f32[16,64]{1,0:T(8,128)} %get-tuple-element.232) | copy-start | bytes 12292
  455.7 35.5 %copy-start.1 = (bf16[1,1,64,1024]{3,2,1,0:T(8,128)(2,1)S(1)}, bf16[1,1,64,1024]{3,2,1,0:T(8,128)(2,1)}, u32[]{:S(2)}) copy-start(bf16[1,1,64,1024]{3,2,1,0:T(8,128)(2,1)} %param.11) | copy-start | bytes 393220
  458.5 32.0 %all-to-all-start.3 = ((bf16[8,8,1024]{2,1,0:T(8,128)(2,1)}), bf16[8,8,1024]{2,1,0:T(8,128)(2,1)S(1)}, u32[]{:S(2)}, u32[]{:S(2)}) async-start(bf16[8,8,1024]{2,1,0:T(8,128)(2,1)} %copy.137), calls=%async_computation.3 | async-start | bytes 262144 | tf_op jit(solution)/shard_map/all_to_all | solution.py:194
  (8 other events, 18.7 us)
Sparse Core Ops, SparseCore 0:
  272.1 38.1 all-gather.10
  312.2 37.3 all-gather.8
  381.5 35.7 all-gather.14
  419.1 36.5 all-gather.12
